TPU v7x, 32 devices: a whole 2x2x4 slice. The times are simulated.
32 devices in a mesh: dp: 8 (over z, y), tensor: 4 (over x, core).
Axes of the slice: x: 2, y: 2, z: 4, core: 2. Of those that a mesh axis runs over, the one named last changes fastest.
Arguments:
- hidden: bfloat16 [1024, 7168], P('dp', 'tensor'), may hold values from -6 to 6
- hash_rows: int32 [1024, 4], P('dp', 'tensor'), may hold values from 0 to 8191, as said below
- memory_table: bfloat16 [8192, 896], P(('dp', 'tensor')), may hold values from -6 to 6
- key_weight: bfloat16 [3584, 7168], P(None, 'tensor'), may hold values from -0.09375 to 0.09375
- value_weight: bfloat16 [3584, 7168], P(None, 'tensor'), may hold values from -0.09375 to 0.09375
- hidden_gain: float32 [7168], P('tensor'), may hold values from 0.1 to 1.9
- key_gain: float32 [7168], P('tensor'), may hold values from 0.1 to 1.9
Outputs:
- joined: bfloat16 [1024, 7168], P('dp', 'tensor')
Inputs may be any that keep to these rules, and one draw needn't show every extreme that they name: `hash_rows`: row r lies in the block of 256 rows held by device r // 256 of dp+tensor. Of the lookups that one device holds (128 requests of its dp group times its 4 / 4 heads), at most 8 fall into any one device's block, and in every draw some device's block receives exactly 8 from every device.
All inputs are finite; a program needn't handle non-finite values.
Results may differ from a plain program's by a relative error of at most 0.0014.
Values may be sent and summed in bfloat16 or wider, within the bound.
A program may use at most 64 MiB of HBM per device.

v0:
```python
import math

import jax
import jax.numpy as jnp
from jax import lax
from jax.sharding import PartitionSpec as P

D = 7168


epsilon = 1e-06


def fetch_rows(row_numbers, capacity, memory_table):
    requests_here = row_numbers.shape[0]
    heads_here = row_numbers.shape[1]
    lookups = requests_here * heads_here
    rows_held = memory_table.shape[0]
    row_width = memory_table.shape[1]
    devices = lax.axis_size("dp") * lax.axis_size("tensor")
    flattened = row_numbers.reshape(lookups)
    owners = flattened // rows_held
    local_rows = flattened - owners * rows_held
    owner_mask = (owners[:, None] == jnp.arange(devices, dtype=jnp.int32)[None, :]).astype(
        jnp.int32
    )
    earlier = jnp.cumsum(owner_mask, axis=0) - owner_mask
    slot_index = jnp.sum(earlier * owner_mask, axis=1)
    position = owners * capacity + slot_index
    wanted = jnp.zeros((devices * capacity,), jnp.int32).at[position].set(local_rows)
    wanted = wanted.reshape(devices, capacity)
    returned = lax.all_to_all(
        memory_table[
            lax.all_to_all(wanted, ("dp", "tensor"), split_axis=0, concat_axis=0, tiled=True)
        ],
        ("dp", "tensor"),
        split_axis=0,
        concat_axis=0,
        tiled=True,
    )
    arrived = returned.reshape(devices * capacity, row_width)
    gathered_rows = arrived[position]
    return gathered_rows


def local(hidden, hash_rows, memory_table, key_weight, value_weight, hidden_gain, key_gain):
    devices = lax.axis_size("dp") * lax.axis_size("tensor")
    base_capacity = 2 * max(1, hash_rows.size // devices)
    memory = fetch_rows(hash_rows, base_capacity, memory_table)
    portion = lax.all_gather(memory, "tensor", axis=1, tiled=True)
    key = jnp.dot(portion, key_weight, preferred_element_type=jnp.float32)
    projected = jnp.dot(portion, value_weight, preferred_element_type=jnp.float32)
    hidden_float = hidden.astype(jnp.float32)
    hidden_scaled = hidden_float * hidden_gain
    key_scaled = key * key_gain
    hidden_squares = jnp.sum(hidden_float * hidden_float, axis=1)
    key_squares = jnp.sum(key * key, axis=1)
    crossing = jnp.sum(hidden_scaled * key_scaled, axis=1)
    hidden_total, key_total, cross_total = lax.psum(
        (hidden_squares, key_squares, crossing), "tensor"
    )
    agreement = (
        cross_total * lax.rsqrt(hidden_total / D + epsilon) * lax.rsqrt(key_total / D + epsilon)
    )
    gate_value = jax.nn.sigmoid(agreement / math.sqrt(D))
    return (hidden_float + gate_value[:, None] * projected).astype(jnp.bfloat16)


def solution(mesh):
    return jax.shard_map(
        local,
        mesh=mesh,
        in_specs=(
            P("dp", "tensor"),
            P("dp", "tensor"),
            P(("dp", "tensor"), None),
            P(None, "tensor"),
            P(None, "tensor"),
            P("tensor"),
            P("tensor"),
        ),
        out_specs=P("dp", "tensor"),
        check_vma=False,
    )
```

profile of v0, /device:TPU:0, one launch (start us, length us, event | category | flops | bytes accessed | tf_op | source)
XLA Modules:
  0.0 67.8 jit_solution(13786215088878763283)
XLA Ops:
  0.0 0.0 copy-start
  0.0 0.7 %fusion.13 = s32[128]{0:T(128)S(1)} fusion(s32[128,1]{0,1:T(1,128)} %param.8), kind=kLoop, calls=%fused_computation.34 | loop fusion | flops 1920 | bytes 1024 | tf_op jit(solution)/shard_map/eq | solution.py:24
  0.7 0.7 bitcast_subtract_fusion
  1.4 0.1 fusion.5
  1.5 0.2 reduce_window_sum.11
  1.6 0.2 select_reduce_fusion
  1.8 0.7 fusion.6
  2.5 1.0 %scatter_custom_fusion = s32[256]{0:T(256)S(1)} fusion(s32[128]{0:T(128)S(1)} %fusion.6, s32[128]{0:T(128)S(1)} %bitcast_subtract_fusion, s32[]{:T(128)} %constant.17.clone.1), kind=kCustom, calls=%fused_computation.32 | custom fusion | bytes 1028 | tf_op jit(solution)/shard_map/scatter | solution.py:30
  3.5 0.1 all_to_all.11
  3.6 14.3 %all_to_all.17 = s32[32,1,8]{2,1,0:T(1,128)S(1)} all-to-all(s32[32,1,8]{2,1,0:T(1,128)S(1)} %bitcast.31), channel_id=1, replica_groups=mesh['dp'=8,'tensor'=4] {'dp','tensor'}, dimensions={0} | all-to-all | bytes 2048 | tf_op jit(solution)/shard_map/all_to_all | solution.py:34
  17.9 0.1 reshape.46
  18.0 0.0 copy-done
  18.0 2.0 %gather_fusion = bf16[256,896]{1,0:T(8,128)(2,1)} fusion(bf16[256,896]{1,0:T(8,128)(2,1)S(1)} %copy-done, s32[1024]{0:T(1024)S(1)} %pad_clamp_fusion.1), kind=kCustom, calls=%fused_computation | custom fusion | bytes 918528 | tf_op jit(solution)/shard_map/gather | solution.py:33
  19.9 0.0 copy-start.1
  19.9 2.7 %all-to-all-start.1 = ((bf16[32,8,896]{2,1,0:T(8,128)(2,1)}), bf16[32,8,896]{2,1,0:T(8,128)(2,1)S(1)}, u32[]{:S(2)}, u32[]{:S(2)}) async-start(bf16[32,8,896]{2,1,0:T(8,128)(2,1)} %bitcast.6), calls=%async_computation.1 | async-start | bytes 917504 | tf_op jit(solution)/shard_map/all_to_all | solution.py:32
  22.7 14.4 %all-to-all-done.1 = bf16[32,8,896]{2,1,0:T(8,128)(2,1)S(1)} async-done(((bf16[32,8,896]{2,1,0:T(8,128)(2,1)}), bf16[32,8,896]{2,1,0:T(8,128)(2,1)S(1)}, u32[]{:S(2)}, u32[]{:S(2)}) %all-to-all-start.1) | async-done | bytes 458784 | tf_op jit(solution)/shard_map/all_to_all | solution.py:32
  37.1 0.9 %gather_fusion.1 = bf16[128,896]{1,0:T(8,128)(2,1)S(1)} fusion(bf16[256,896]{1,0:T(8,128)(2,1)S(1)} %bitcast.30, s32[1024]{0:T(1024)S(1)} %pad_clamp_fusion), kind=kCustom, calls=%fused_computation.1 | custom fusion | bytes 459264 | tf_op jit(solution)/shard_map/gather | solution.py:42
  38.0 8.8 %all-gather = bf16[128,3584]{1,0:T(8,128)(2,1)S(1)} all-gather(bf16[128,896]{1,0:T(8,128)(2,1)S(1)} %gather_fusion.1), channel_id=2, replica_groups=mesh['dp'=8,'tensor'=4] {'tensor'}, dimensions={1}, use_global_device_ids=true | all-gather | bytes 1146880 | tf_op jit(solution)/shard_map/all_gather | solution.py:50
  46.8 6.8 %fusion.3 = (f32[128]{0:T(128)S(1)}, f32[128]{0:T(128)S(1)}, f32[128]{0:T(128)S(1)}) fusion(bf16[128,1792]{1,0:T(8,128)(2,1)} %param.7, f32[1792]{0:T(1024)} %param.13, f32[1792]{0:T(1024)} %param.12, bf16[128,3584]{1,0:T(8,128)(2,1)S(1)} %all-gather, bf16[3584,1792]{1,0:T(8,128)(2,1)} %param.10), kind=kOutput, calls=%fused_computation.9 | convolution fusion | flops 1646231168 | bytes 14237184 | tf_op jit(solution)/shard_map/dot_general | solution.py:51
  53.6 6.9 %all-reduce = (f32[128]{0:T(128)S(1)}, f32[128]{0:T(128)S(1)}, f32[128]{0:T(128)S(1)}) all-reduce(f32[128]{0:T(128)S(1)} %get-tuple-element.6, f32[128]{0:T(128)S(1)} %get-tuple-element.5, f32[128]{0:T(128)S(1)} %get-tuple-element.7), channel_id=1, replica_groups=mesh['dp'=8,'tensor'=4] {'tensor'}, use_global_device_ids=true, to_apply=%region_8.9 | all-reduce | flops 384 | bytes 3072 | tf_op jit(solution)/shard_map/psum | solution.py:59
  60.6 0.0 copy-done.1
  60.6 7.3 %fusion.1 = bf16[128,1792]{1,0:T(8,128)(2,1)} fusion(bf16[128,3584]{1,0:T(8,128)(2,1)S(1)} %all-gather, bf16[3584,1792]{1,0:T(8,128)(2,1)} %param.11, bf16[128,1792]{1,0:T(8,128)(2,1)S(1)} %copy-done.1, f32[128]{0:T(128)S(1)} %add_divide_fusion), kind=kOutput, calls=%fused_computation.5 | convolution fusion | flops 1645084672 | bytes 14680576 | tf_op jit(solution)/shard_map/dot_general | solution.py:52
  (4 shorter events, 0.0 us)
Async XLA Ops:
  0.0 18.0 %copy-start = (bf16[256,896]{1,0:T(8,128)(2,1)S(1)}, bf16[256,896]{1,0:T(8,128)(2,1)}, u32[]{:S(2)}) copy-start(bf16[256,896]{1,0:T(8,128)(2,1)} %param.9) | copy-start | bytes 1376260
  19.9 40.6 %copy-start.1 = (bf16[128,1792]{1,0:T(8,128)(2,1)S(1)}, bf16[128,1792]{1,0:T(8,128)(2,1)}, u32[]{:S(2)}) copy-start(bf16[128,1792]{1,0:T(8,128)(2,1)} %param.7) | copy-start | bytes 1376260
  19.9 17.2 %all-to-all-start.1 = ((bf16[32,8,896]{2,1,0:T(8,128)(2,1)}), bf16[32,8,896]{2,1,0:T(8,128)(2,1)S(1)}, u32[]{:S(2)}, u32[]{:S(2)}) async-start(bf16[32,8,896]{2,1,0:T(8,128)(2,1)} %bitcast.6), calls=%async_computation.1 | async-start | bytes 917504 | tf_op jit(solution)/shard_map/all_to_all | solution.py:32
where the time goes:
time: 68.1 us; the launch traced here: 67.8 us
  blocking collectives  30 us (44%)
  waiting for transfers between devices  14.4 us (21%)
  matrix products  14.1 us (21%)
  local copies, waits for them, and re-layouts  3.98 us (6%)
  starting transfers between devices  2.73 us (4%)
  other arithmetic  2.52 us (4%)
    all_to_all x1, waiting for transfers between devices, fetch_rows(): lax.all_to_all(memory_table[lax.all_to_all(wanted, ('dp', 'tensor'), spli...  14.4 us
    all_to_all x1, blocking collectives, fetch_rows(): lax.all_to_all(wanted, ('dp', 'tensor'), split_axis=0, concat_axis=0, til...  14.3 us
    all_gather x1, blocking collectives, local(): portion = lax.all_gather(memory, 'tensor', axis=1, tiled=True)  8.78 us
    dot_general x1, matrix products, local(): jnp.dot(portion, value_weight, preferred_element_type=jnp.float32)  7.26 us
    psum x1, blocking collectives, local(): lax.psum((hidden_squares, key_squares, crossing), 'tensor')  6.95 us
    dot_general x1, matrix products, local(): key = jnp.dot(portion, key_weight, preferred_element_type=jnp.float32)  6.81 us
    all_to_all x1, starting transfers between devices, fetch_rows(): lax.all_to_all(memory_table[lax.all_to_all(wanted, ('dp', 'tensor'), spli...  2.73 us
    gather x1, local copies, waits for them, and re-layouts, fetch_rows(): memory_table[lax.all_to_all(wanted, ('dp', 'tensor'), split_axis=0, conca...  1.95 us
  transfers between devices with their start and end apart: 1, of which 1 were waited for; matrix products, arithmetic and copies ran while one was open for 0% of the time, Pallas kernels for 0%

commit v1 on v0

v1 whole, which is shorter than its diff:
```python
import functools
import math

import jax
import jax.numpy as jnp
from jax import lax
from jax.experimental import pallas as pl
from jax.experimental.pallas import tpu as pltpu
from jax.sharding import PartitionSpec as P

MESH = pl.DeviceIdType.MESH
epsilon = 1e-06
F32, BF16 = jnp.float32, jnp.bfloat16


def dot(a, b):
    return jnp.dot(a, b, preferred_element_type=F32)


def kernel(groups, heads, slots, ids_ref, hg_ref, kg_ref, table_hbm, hidden_hbm, wk_hbm, wv_hbm, out_ref,
           ids, table, hidden, wk, wv, sending, rows, place, mem, acc_k, acc_v, stats,
           local_sem, w_sem, own_sem, id_send, id_recv, list_send, list_recv,
           row_send, row_recv, pass_send, pass_recv, stat_send, stat_recv):
    me_p, me_t = lax.axis_index("dp"), lax.axis_index("tensor")
    held, width = table.shape
    requests, columns = hidden.shape
    model = columns * heads
    chunk = 256 if columns % 256 == 0 else 128

    def here(source, target, sem):
        return pltpu.make_async_copy(source, target, sem)

    def there(source, target, send, recv, p, t):
        return pltpu.make_async_remote_copy(
            src_ref=source, dst_ref=target, send_sem=send, recv_sem=recv,
            device_id={"dp": p, "tensor": t}, device_id_type=MESH)

    def ahead(i):
        return lax.rem(me_p + i, groups)

    def behind(i):
        return lax.rem(me_p + groups - i, groups)

    own_ids = here(ids_ref.at[0], ids.at[me_p, me_t], local_sem.at[0])
    own_ids.start()
    table_copy = here(table_hbm, table, local_sem.at[1])
    table_copy.start()
    weights = []
    for h in range(heads):
        for which, (source, target) in enumerate(((wk_hbm, wk), (wv_hbm, wv))):
            copy = here(source.at[pl.ds(h * width, width), :], target.at[h], w_sem.at[h, which])
            copy.start()
            weights.append(copy)
    hidden_copy = here(hidden_hbm, hidden, local_sem.at[2])
    hidden_copy.start()

    barrier = pltpu.get_barrier_semaphore()

    @pl.loop(1, groups)
    def _(i):
        pl.semaphore_signal(barrier, inc=1, device_id={"dp": ahead(i), "tensor": me_t}, device_id_type=MESH)

    for m in range(1, heads):
        pl.semaphore_signal(barrier, inc=1, device_id={"dp": me_p, "tensor": me_t ^ m}, device_id_type=MESH)
    pl.semaphore_wait(barrier, groups - 1 + heads - 1)

    def id_copy(m, t):
        return there(ids_ref.at[0], ids.at[me_p, t], id_send.at[m - 1], id_recv.at[m - 1], me_p, me_t ^ m)

    for m in range(1, heads):
        id_copy(m, me_t).start()
    own_ids.wait()
    for m in range(1, heads):
        id_copy(m, me_t ^ m).wait_recv()

    def list_copy(i, p):
        return there(ids.at[me_p], ids.at[p], list_send.at[i - 1], list_recv.at[i - 1], ahead(i), me_t)

    @pl.loop(1, groups)
    def _(i):
        list_copy(i, me_p).start()

    sub = lax.broadcasted_iota(jnp.int32, (requests, requests), 0)
    lane = lax.broadcasted_iota(jnp.int32, (requests, requests), 1)
    spots = lax.broadcasted_iota(jnp.int32, (requests, groups * heads * slots), 1).astype(F32)
    for h in range(heads):
        numbers = ids[me_p, h].astype(F32)
        owner = jnp.broadcast_to(jnp.floor((numbers + 0.5) * (1.0 / held)), (requests, requests))
        column = jnp.sum(jnp.where(sub == lane, owner, 0.0), axis=1, keepdims=True)
        rank = jnp.sum(jnp.where((owner == column) & (lane < sub), 1.0, 0.0), axis=1, keepdims=True)
        owner_p = jnp.floor((column + 0.5) * (1.0 / heads))
        owner_t = column - owner_p * heads
        spot = (owner_t * groups + owner_p) * slots + rank
        place[h] = jnp.where(spots == spot, 1.0, 0.0).astype(BF16)

    hidden_copy.wait()
    hidden_squares = jnp.zeros((requests, 1), F32)
    for c in range(columns // chunk):
        part = hidden[:, c * chunk:(c + 1) * chunk].astype(F32)
        hidden_squares += jnp.sum(part * part, axis=1, keepdims=True)

    @pl.loop(1, groups)
    def _(i):
        list_copy(i, behind(i)).wait_recv()

    lists = jnp.concatenate([ids[:, h].reshape(groups, requests) for h in range(heads)], axis=0)
    first = (me_p * heads + me_t) * held
    mine = (lists >= first) & (lists < first + held)
    earlier = jnp.where(sub < lane, 1.0, 0.0).astype(BF16)
    order = dot(jnp.where(mine, 1.0, 0.0).astype(BF16), earlier)
    order = jnp.where(mine, order, -1.0).astype(BF16)
    local = jnp.where(mine, lists - first, 0).astype(F32).astype(BF16)
    total = heads * groups * slots
    row = lax.broadcasted_iota(jnp.int32, (total, heads * groups), 0)
    source = lax.broadcasted_iota(jnp.int32, (total, heads * groups), 1) * slots
    spread = jnp.where((row >= source) & (row < source + slots), 1.0, 0.0).astype(BF16)
    slot = (lax.broadcasted_iota(jnp.int32, (total, requests), 0) & (slots - 1)).astype(F32)
    wanted = jnp.sum(jnp.where(dot(spread, order) == slot, dot(spread, local), 0.0), axis=1, keepdims=True)
    choose = jnp.where(
        lax.broadcasted_iota(jnp.int32, (total, held), 1).astype(F32) == wanted, 1.0, 0.0).astype(BF16)
    table_copy.wait()

    def row_copy(h, i, p):
        return there(sending.at[h, ahead(i)], rows.at[h, me_t, p],
                     row_send.at[h, i - 1], row_recv.at[h, i - 1], ahead(i), me_t)

    per_head = groups * slots
    for h in range(heads):
        block = dot(choose[h * per_head:(h + 1) * per_head], table[...])
        sending[h] = block.reshape(groups, slots, width).astype(BF16)

        @pl.loop(1, groups)
        def _(i):
            row_copy(h, i, me_p).start()

        here(sending.at[h, me_p], rows.at[h, me_t, me_p], own_sem.at[h]).start()

    def pass_on(h, bit, m, t):
        return there(rows.at[h, me_t ^ m], rows.at[h, t], pass_send.at[h, (m | bit) - 1],
                     pass_recv.at[h, (m | bit) - 1], me_p, me_t ^ bit)

    bits, bit = [], heads // 2
    while bit:
        bits.append(bit)
        bit //= 2

    def begin(h):
        here(sending.at[h, me_p], rows.at[h, me_t, me_p], own_sem.at[h]).wait()

        @pl.loop(1, groups)
        def _(i):
            row_copy(h, i, behind(i)).wait_recv()

        for b in bits:
            pass_on(h, b, 0, me_t).start()

    def onward(h):
        masks = [0]
        for n, b in enumerate(bits):
            if n:
                for m in masks[1:]:
                    pass_on(h, b, m, me_t ^ m).start()
            if n < len(bits) - 1:
                for m in masks:
                    pass_on(h, b, m, me_t ^ m ^ b).wait_recv()
            masks = masks + [m | b for m in masks]

    def finish(h):
        b = bits[-1]
        for m in range(0, heads, 2):
            pass_on(h, b, m, me_t ^ m ^ b).wait_recv()

    def multiply(h):
        finish(h)
        mem[...] = dot(place[h], rows[h].reshape(groups * heads * slots, width)).astype(BF16)
        weights[2 * h].wait()
        weights[2 * h + 1].wait()

        @pl.loop(0, columns // chunk)
        def _(c):
            part = pl.ds(pl.multiple_of(c * chunk, chunk), chunk)
            for w, acc in ((wk, acc_k), (wv, acc_v)):
                value = dot(mem[...], w[h, :, part])
                acc[:, part] = value if h == 0 else acc[:, part] + value

    for h in range(heads):
        begin(h)
        if h:
            multiply(h - 1)
        onward(h)
    multiply(heads - 1)

    key_squares = jnp.zeros((requests, 1), F32)
    crossing = jnp.zeros((requests, 1), F32)
    for c in range(columns // chunk):
        part = slice(c * chunk, (c + 1) * chunk)
        key = acc_k[:, part]
        key_squares += jnp.sum(key * key, axis=1, keepdims=True)
        scaled = hidden[:, part].astype(F32) * hg_ref[:, part] * (key * kg_ref[:, part])
        crossing += jnp.sum(scaled, axis=1, keepdims=True)
    lanes = lax.broadcasted_iota(jnp.int32, (requests, 128), 1)
    packed = jnp.where(lanes == 0, hidden_squares, jnp.where(lanes == 1, key_squares,
                       jnp.where(lanes == 2, crossing, 0.0)))
    stats[0] = packed.T[:8]

    def stat_copy(m):
        return there(stats.at[0], stats.at[m], stat_send.at[m - 1], stat_recv.at[m - 1], me_p, me_t ^ m)

    for m in range(1, heads):
        stat_copy(m).start()
    for m in range(1, heads):
        stat_copy(m).wait_recv()
    summed = stats[0]
    for m in range(1, heads):
        summed += stats[m]
    turned = jnp.concatenate([summed, jnp.zeros((120, requests), F32)], axis=0).T
    hidden_total, key_total, cross_total = turned[:, 0:1], turned[:, 1:2], turned[:, 2:3]
    agreement = (cross_total * lax.rsqrt(hidden_total / model + epsilon)
                 * lax.rsqrt(key_total / model + epsilon))
    gate = jax.nn.sigmoid(agreement / math.sqrt(model))
    for c in range(columns // chunk):
        part = slice(c * chunk, (c + 1) * chunk)
        out_ref[:, part] = (hidden[:, part].astype(F32) + gate * acc_v[:, part]).astype(BF16)

    for m in range(1, heads):
        id_copy(m, me_t).wait_send()
        stat_copy(m).wait_send()

    @pl.loop(1, groups)
    def _(i):
        list_copy(i, me_p).wait_send()
        for h in range(heads):
            row_copy(h, i, me_p).wait_send()

    for h in range(heads):
        masks = [0]
        for b in bits:
            for m in masks:
                pass_on(h, b, m, me_t ^ m).wait_send()
            masks = masks + [m | b for m in masks]


def local(groups, heads, hidden, hash_rows, memory_table, key_weight, value_weight, hidden_gain, key_gain):
    requests, columns = hidden.shape
    held, width = memory_table.shape
    assert hash_rows.shape[1] == 1 and heads & (heads - 1) == 0 and heads > 1
    slots = max(8, 2 * max(1, hash_rows.size // (groups * heads)))
    any_space = pl.BlockSpec(memory_space=pl.ANY)
    vmem = pl.BlockSpec(memory_space=pltpu.VMEM)
    dma = pltpu.SemaphoreType.DMA
    return pl.pallas_call(
        functools.partial(kernel, groups, heads, slots),
        out_shape=jax.ShapeDtypeStruct((requests, columns), BF16),
        in_specs=[vmem] * 3 + [any_space] * 4,
        out_specs=vmem,
        scratch_shapes=[
            pltpu.VMEM((groups, heads, 1, requests), jnp.int32),
            pltpu.VMEM((held, width), BF16),
            pltpu.VMEM((requests, columns), BF16),
            pltpu.VMEM((heads, width, columns), BF16),
            pltpu.VMEM((heads, width, columns), BF16),
            pltpu.VMEM((heads, groups, slots, width), BF16),
            pltpu.VMEM((heads, heads, groups, slots, width), BF16),
            pltpu.VMEM((heads, requests, groups * heads * slots), BF16),
            pltpu.VMEM((requests, width), BF16),
            pltpu.VMEM((requests, columns), F32),
            pltpu.VMEM((requests, columns), F32),
            pltpu.VMEM((heads, 8, requests), F32),
            dma((3,)), dma((heads, 2)), dma((heads,)),
            dma((heads - 1,)), dma((heads - 1,)),
            dma((groups - 1,)), dma((groups - 1,)),
            dma((heads, groups - 1)), dma((heads, groups - 1)),
            dma((heads, heads - 1)), dma((heads, heads - 1)),
            dma((heads - 1,)), dma((heads - 1,)),
        ],
        compiler_params=pltpu.CompilerParams(
            collective_id=0, has_side_effects=True, vmem_limit_bytes=60 * 1024 * 1024),
    )(hash_rows.reshape(1, 1, requests), hidden_gain.reshape(1, columns), key_gain.reshape(1, columns),
      memory_table, hidden, key_weight, value_weight)


def solution(mesh):
    return jax.shard_map(
        functools.partial(local, mesh.shape["dp"], mesh.shape["tensor"]),
        mesh=mesh,
        in_specs=(
            P("dp", "tensor"),
            P("dp", "tensor"),
            P(("dp", "tensor"), None),
            P(None, "tensor"),
            P(None, "tensor"),
            P("tensor"),
            P("tensor"),
        ),
        out_specs=P("dp", "tensor"),
        check_vma=False,
    )
```

time: 68.1 us -> 48 us (0.70)
  Pallas kernels: 0 us -> 42.7 us
  blocking collectives: 30 us -> 0 us
  waiting for transfers between devices: 14.4 us -> 0 us
  matrix products: 14.1 us -> 0 us
  starting transfers between devices: 2.73 us -> 0 us
  other arithmetic: 2.52 us -> 0 us
    pallas_call x0 -> x1, Pallas kernels: none -> 42.7 us  [local(): pl.pallas_call(functools.partial(kernel, groups, heads, slots), out_shape...]
    all_to_all x1 -> x0, waiting for transfers between devices: 14.4 us -> none  [fetch_rows(): lax.all_to_all(memory_table[lax.all_to_all(wanted, ('dp', 'tensor'), spli...]
    all_to_all x1 -> x0, blocking collectives: 14.3 us -> none  [fetch_rows(): lax.all_to_all(wanted, ('dp', 'tensor'), split_axis=0, concat_axis=0, til...]
    dot_general x2 -> x0, matrix products: 14.1 us -> none  [the longest x1 7.26 us: local(): jnp.dot(portion, value_weight, preferred_element_type=jnp.float32)]
    all_gather x1 -> x0, blocking collectives: 8.78 us -> none  [local(): portion = lax.all_gather(memory, 'tensor', axis=1, tiled=True)]
    psum x1 -> x0, blocking collectives: 6.95 us -> none  [local(): lax.psum((hidden_squares, key_squares, crossing), 'tensor')]
    gather x2 -> x0, local copies, waits for them, and re-layouts: 2.83 us -> none  [the longest x1 1.95 us: fetch_rows(): memory_table[lax.all_to_all(wanted, ('dp', 'tensor'), split_axis=0, conca...]
    all_to_all x1 -> x0, starting transfers between devices: 2.73 us -> none  [fetch_rows(): lax.all_to_all(memory_table[lax.all_to_all(wanted, ('dp', 'tensor'), spli...]
  transfers between devices with their start and end apart: 1 -> 0, of which waited for: 1 -> 0; matrix products, arithmetic and copies ran while one was open for 0% -> 0% of each run, Pallas kernels for 0% -> 0%
where the time goes in v1:
time: 48 us; the launch traced here: 47.2 us
  Pallas kernels  42.7 us (89%)
  local copies, waits for them, and re-layouts  4.4 us (9%)
    pallas_call x1, Pallas kernels, local(): pl.pallas_call(functools.partial(kernel, groups, heads, slots), out_shape...  42.7 us
    unnamed x1, local copies, waits for them, and re-layouts  1.82 us
    reshape x1, local copies, waits for them, and re-layouts, local(): hidden_gain.reshape(1, columns)  1.29 us
    reshape x1, local copies, waits for them, and re-layouts, local(): key_gain.reshape(1, columns)  1.29 us

profile of v1, /device:TPU:0, one launch (start us, length us, event | category | flops | bytes accessed | tf_op | source)
XLA Modules:
  0.0 47.2 jit_solution(14609225289703034222)
XLA Ops:
  0.0 1.3 %reshape.10.hg_ref = f32[1,1792]{1,0:T(1,128)} reshape(f32[1792]{0:T(1024)} %param.12) | data formatting | bytes 14336 | tf_op jit(solution)/shard_map/reshape | solution.py:278
  1.3 1.3 %reshape.11.kg_ref = f32[1,1792]{1,0:T(1,128)} reshape(f32[1792]{0:T(1024)} %param.13) | data formatting | bytes 14336 | tf_op jit(solution)/shard_map/reshape | solution.py:278
  2.6 42.7 %shard_map.73 = bf16[128,1792]{1,0:T(8,128)(2,1)} custom-call(s32[1,1,128]{2,1,0:T(1,128)} %bitcast.1, f32[1,1792]{1,0:T(1,128)} %reshape.10.hg_ref, f32[1,1792]{1,0:T(1,128)} %reshape.11.kg_ref, bf16[256,896]{1,0:T(8,128)(2,1)} %table_hbm.1, bf16[128,1792]{1,0:T(8,128)(2,1)} %hidden_hbm.1, bf16[3584,1792]{1,0:T(8,128)(2,1)} %wk_hbm.1, bf16[3584,1792]{1,0:T(8,128)(2,1)} %wv_hbm.1), custom_call_target="tpu_custom_call" | custom-call | tf_op jit(solution)/shard_map/pallas_call | solution.py:251
  45.3 1.8 %copy.9 = bf16[128,1792]{1,0:T(8,128)(2,1)} copy(bf16[128,1792]{1,0:T(8,128)(2,1)} %shard_map.73) | data formatting | bytes 917504

commit v2 on v1

--- a/solution.py
+++ b/solution.py
@@ -124,16 +124,18 @@
         return there(sending.at[h, ahead(i)], rows.at[h, me_t, p],
                      row_send.at[h, i - 1], row_recv.at[h, i - 1], ahead(i), me_t)
 
+    def send_rows(h):
+        @pl.loop(1, groups)
+        def _(i):
+            row_copy(h, i, me_p).start()
+
     per_head = groups * slots
     for h in range(heads):
         block = dot(choose[h * per_head:(h + 1) * per_head], table[...])
         sending[h] = block.reshape(groups, slots, width).astype(BF16)
-
-        @pl.loop(1, groups)
-        def _(i):
-            row_copy(h, i, me_p).start()
-
         here(sending.at[h, me_p], rows.at[h, me_t, me_p], own_sem.at[h]).start()
+        if h < 2:
+            send_rows(h)
 
     def pass_on(h, bit, m, t):
         return there(rows.at[h, me_t ^ m], rows.at[h, t], pass_send.at[h, (m | bit) - 1],
@@ -153,6 +155,8 @@
 
         for b in bits:
             pass_on(h, b, 0, me_t).start()
+        if h + 2 < heads:
+            send_rows(h + 2)
 
     def onward(h):
         masks = [0]
@@ -183,12 +187,13 @@
                 value = dot(mem[...], w[h, :, part])
                 acc[:, part] = value if h == 0 else acc[:, part] + value
 
-    for h in range(heads):
-        begin(h)
-        if h:
-            multiply(h - 1)
-        onward(h)
-    multiply(heads - 1)
+    for step in range(heads + 2):
+        if step < heads:
+            begin(step)
+        if step > 1:
+            multiply(step - 2)
+        if 0 < step <= heads:
+            onward(step - 1)
 
     key_squares = jnp.zeros((requests, 1), F32)
     crossing = jnp.zeros((requests, 1), F32)
@@ -196,7 +201,7 @@
         part = slice(c * chunk, (c + 1) * chunk)
         key = acc_k[:, part]
         key_squares += jnp.sum(key * key, axis=1, keepdims=True)
-        scaled = hidden[:, part].astype(F32) * hg_ref[:, part] * (key * kg_ref[:, part])
+        scaled = hidden[:, part].astype(F32) * hg_ref[part].reshape(1, chunk) * (key * kg_ref[part].reshape(1, chunk))
         crossing += jnp.sum(scaled, axis=1, keepdims=True)
     lanes = lax.broadcasted_iota(jnp.int32, (requests, 128), 1)
     packed = jnp.where(lanes == 0, hidden_squares, jnp.where(lanes == 1, key_squares,
@@ -275,7 +280,7 @@
         ],
         compiler_params=pltpu.CompilerParams(
             collective_id=0, has_side_effects=True, vmem_limit_bytes=60 * 1024 * 1024),
-    )(hash_rows.reshape(1, 1, requests), hidden_gain.reshape(1, columns), key_gain.reshape(1, columns),
+    )(hash_rows.reshape(1, 1, requests), hidden_gain, key_gain,
       memory_table, hidden, key_weight, value_weight)
 
 

time: 48 us -> 43.6 us (0.908); the launches traced: 47.2 us -> 43.4 us
  local copies, waits for them, and re-layouts: 4.4 us -> 1.82 us
  Pallas kernels: 42.7 us -> 41.6 us
    reshape x2 -> x0, local copies, waits for them, and re-layouts: 2.59 us -> none  [the longest x1 1.29 us: local(): hidden_gain.reshape(1, columns)]
    pallas_call x1, Pallas kernels: 42.7 us -> 41.6 us  [local(): pl.pallas_call(functools.partial(kernel, groups, heads, slots), out_shape...]
where the time goes in v2:
time: 43.6 us; the launch traced here: 43.4 us
  Pallas kernels  41.6 us (95%)
  local copies, waits for them, and re-layouts  1.82 us (4%)
    pallas_call x1, Pallas kernels, local(): pl.pallas_call(functools.partial(kernel, groups, heads, slots), out_shape...  41.6 us
    unnamed x1, local copies, waits for them, and re-layouts  1.82 us

profile of v2, /device:TPU:0, one launch (start us, length us, event | category | flops | bytes accessed | tf_op | source)
XLA Modules:
  0.0 43.4 jit_solution(8674958579795283076)
XLA Ops:
  0.0 41.6 %shard_map.73 = bf16[128,1792]{1,0:T(8,128)(2,1)} custom-call(s32[1,1,128]{2,1,0:T(1,128)} %bitcast.1, f32[1792]{0:T(1024)} %hg_ref.1, f32[1792]{0:T(1024)} %kg_ref.1, bf16[256,896]{1,0:T(8,128)(2,1)} %table_hbm.1, bf16[128,1792]{1,0:T(8,128)(2,1)} %hidden_hbm.1, bf16[3584,1792]{1,0:T(8,128)(2,1)} %wk_hbm.1, bf16[3584,1792]{1,0:T(8,128)(2,1)} %wv_hbm.1), custom_call_target="tpu_custom_call" | custom-call | tf_op jit(solution)/shard_map/pallas_call | solution.py:256
  41.6 1.8 %copy.9 = bf16[128,1792]{1,0:T(8,128)(2,1)} copy(bf16[128,1792]{1,0:T(8,128)(2,1)} %shard_map.73) | data formatting | bytes 917504

commit v3 on v2

--- a/solution.py
+++ b/solution.py
@@ -180,9 +180,8 @@
         weights[2 * h].wait()
         weights[2 * h + 1].wait()
 
-        @pl.loop(0, columns // chunk)
-        def _(c):
-            part = pl.ds(pl.multiple_of(c * chunk, chunk), chunk)
+        for c in range(columns // chunk):
+            part = pl.ds(c * chunk, chunk)
             for w, acc in ((wk, acc_k), (wv, acc_v)):
                 value = dot(mem[...], w[h, :, part])
                 acc[:, part] = value if h == 0 else acc[:, part] + value

time: 43.6 us -> 39.1 us (0.90)
  Pallas kernels: 41.6 us -> 37.1 us
    pallas_call x1, Pallas kernels: 41.6 us -> 37.1 us  [local(): pl.pallas_call(functools.partial(kernel, groups, heads, slots), out_shape...]
where the time goes in v3:
time: 39.1 us; the launch traced here: 38.9 us
  Pallas kernels  37.1 us (95%)
  local copies, waits for them, and re-layouts  1.82 us (5%)
    pallas_call x1, Pallas kernels, local(): pl.pallas_call(functools.partial(kernel, groups, heads, slots), out_shape...  37.1 us
    unnamed x1, local copies, waits for them, and re-layouts  1.82 us

profile of v3, /device:TPU:0, one launch (start us, length us, event | category | flops | bytes accessed | tf_op | source)
XLA Modules:
  0.0 38.9 jit_solution(12281357742507799103)
XLA Ops:
  0.0 37.1 %shard_map.73 = bf16[128,1792]{1,0:T(8,128)(2,1)} custom-call(s32[1,1,128]{2,1,0:T(1,128)} %bitcast.1, f32[1792]{0:T(1024)} %hg_ref.1, f32[1792]{0:T(1024)} %kg_ref.1, bf16[256,896]{1,0:T(8,128)(2,1)} %table_hbm.1, bf16[128,1792]{1,0:T(8,128)(2,1)} %hidden_hbm.1, bf16[3584,1792]{1,0:T(8,128)(2,1)} %wk_hbm.1, bf16[3584,1792]{1,0:T(8,128)(2,1)} %wv_hbm.1), custom_call_target="tpu_custom_call" | custom-call | tf_op jit(solution)/shard_map/pallas_call | solution.py:255
  37.1 1.8 %copy.9 = bf16[128,1792]{1,0:T(8,128)(2,1)} copy(bf16[128,1792]{1,0:T(8,128)(2,1)} %shard_map.73) | data formatting | bytes 917504

commit v4 on v3

--- a/solution.py
+++ b/solution.py
@@ -134,7 +134,7 @@
         block = dot(choose[h * per_head:(h + 1) * per_head], table[...])
         sending[h] = block.reshape(groups, slots, width).astype(BF16)
         here(sending.at[h, me_p], rows.at[h, me_t, me_p], own_sem.at[h]).start()
-        if h < 2:
+        if h < 3:
             send_rows(h)
 
     def pass_on(h, bit, m, t):
@@ -155,8 +155,8 @@
 
         for b in bits:
             pass_on(h, b, 0, me_t).start()
-        if h + 2 < heads:
-            send_rows(h + 2)
+        if h + 3 < heads:
+            send_rows(h + 3)
 
     def onward(h):
         masks = [0]

time: 39.1 us -> 39.8 us (1.018)
  Pallas kernels: 37.1 us -> 37.7 us
    pallas_call x1, Pallas kernels: 37.1 us -> 37.7 us  [local(): pl.pallas_call(functools.partial(kernel, groups, heads, slots), out_shape...]
where the time goes in v4:
time: 39.8 us; the launch traced here: 39.5 us
  Pallas kernels  37.7 us (95%)
  local copies, waits for them, and re-layouts  1.82 us (5%)
    pallas_call x1, Pallas kernels, local(): pl.pallas_call(functools.partial(kernel, groups, heads, slots), out_shape...  37.7 us
    unnamed x1, local copies, waits for them, and re-layouts  1.82 us

profile of v4, /device:TPU:0, one launch (start us, length us, event | category | flops | bytes accessed | tf_op | source)
XLA Modules:
  0.0 39.5 jit_solution(9306323950382021044)
XLA Ops:
  0.0 37.7 %shard_map.73 = bf16[128,1792]{1,0:T(8,128)(2,1)} custom-call(s32[1,1,128]{2,1,0:T(1,128)} %bitcast.1, f32[1792]{0:T(1024)} %hg_ref.1, f32[1792]{0:T(1024)} %kg_ref.1, bf16[256,896]{1,0:T(8,128)(2,1)} %table_hbm.1, bf16[128,1792]{1,0:T(8,128)(2,1)} %hidden_hbm.1, bf16[3584,1792]{1,0:T(8,128)(2,1)} %wk_hbm.1, bf16[3584,1792]{1,0:T(8,128)(2,1)} %wv_hbm.1), custom_call_target="tpu_custom_call" | custom-call | tf_op jit(solution)/shard_map/pallas_call | solution.py:255
  37.7 1.8 %copy.9 = bf16[128,1792]{1,0:T(8,128)(2,1)} copy(bf16[128,1792]{1,0:T(8,128)(2,1)} %shard_map.73) | data formatting | bytes 917504
